TPU v7x, 256 devices: a whole 4x4x8 slice. The times are simulated.
256 devices in a mesh: seq: 32 (over y, z), head: 4 (over x), dp: 2 (over core).
Axes of the slice: x: 4, y: 4, z: 8, core: 2. Of those that a mesh axis runs over, the one named last changes fastest.
Arguments:
- tokens: bfloat16 [65536, 2048], P(('dp', 'seq', 'head')), parts along dimension 0, may hold values from -6 to 6
- qkv_weight: bfloat16 [2048, 3, 2048], P(None, None, 'head'), may hold values from -0.125 to 0.125
- out_weight: bfloat16 [2048, 2048], P('head'), may hold values from -0.125 to 0.125
- prefix_state: float32 [32, 128, 128], P(('dp', 'head')), parts along dimension 0, may hold values from -1536 to 1536
Outputs:
- layer_out: bfloat16 [65536, 2048], P(('dp', 'seq', 'head')), parts along dimension 0
There are 2 independent parts, one for each index of `dp`. A program takes and returns all parts, laid end to end along the dimension named above; an argument that names none is the same for every part. Nothing has to cross between parts.
All inputs are finite; a program needn't handle non-finite values.
Results may differ from a plain program's by a relative error of at most 0.014.
Values may be sent and summed in bfloat16 or wider, within the bound.
A program may use at most 64 MiB of HBM per device.

v0:
```python
import jax
import jax.numpy as jnp
from jax import lax
from jax.sharding import PartitionSpec as P


def on_device(tokens, qkv_weight, out_weight, prefix_state):
    model_width = qkv_weight.shape[0]
    head_size = prefix_state.shape[1]
    group_heads = prefix_state.shape[0]
    group_width = group_heads * head_size
    flat = qkv_weight.reshape(model_width, 3 * group_width)
    projected = jnp.dot(
        lax.all_gather(tokens, "head", axis=0, tiled=True), flat, preferred_element_type=jnp.float32
    ).astype(jnp.bfloat16)
    length = projected.shape[0]
    query = projected[:, :group_width].reshape(length, group_heads, head_size)
    keys = projected[:, group_width : 2 * group_width].reshape(length, group_heads, head_size)
    values = projected[:, 2 * group_width :].reshape(length, group_heads, head_size)
    local_state = jnp.einsum("thd,the->hde", keys, values, preferred_element_type=jnp.float32)
    my_block = lax.axis_index("seq")
    piece = lax.all_gather(
        local_state[None].astype(jnp.bfloat16), "seq", axis=0, tiled=True
    ).astype(jnp.float32)
    count = piece.shape[0]
    keep = (jnp.arange(count) < my_block).astype(jnp.float32)
    carried = prefix_state + jnp.sum(piece * keep[:, None, None, None], axis=0)
    carried_low = carried.astype(jnp.bfloat16)
    block = min(512, length)
    pieces = []
    for number in range(length // block):
        lower = number * block
        upper = lower + block
        block_q = query[lower:upper]
        scores = jnp.einsum(
            "shd,thd->hst", block_q, keys[:upper], preferred_element_type=jnp.float32
        )
        causal = (lower + jnp.arange(block))[:, None] >= jnp.arange(upper)[None, :]
        weights = jnp.where(causal[None], scores, 0.0).astype(jnp.bfloat16)
        mixed = jnp.einsum(
            "hst,thd->shd", weights, values[:upper], preferred_element_type=jnp.float32
        )
        mixed = mixed + jnp.einsum(
            "shd,hde->she", block_q, carried_low, preferred_element_type=jnp.float32
        )
        factor = lax.rsqrt(jnp.mean(mixed * mixed, axis=-1, keepdims=True) + 1e-06)
        pieces.append((mixed * factor).astype(jnp.bfloat16).reshape(block, group_width))
    normed = jnp.concatenate(pieces, axis=0)
    summed = lax.psum_scatter(
        jnp.dot(normed, out_weight, preferred_element_type=jnp.float32).astype(jnp.bfloat16),
        "head",
        scatter_dimension=0,
        tiled=True,
    ).astype(jnp.float32)
    return (tokens.astype(jnp.float32) + summed).astype(jnp.bfloat16)


def solution(mesh):
    return jax.shard_map(
        on_device,
        mesh=mesh,
        in_specs=(
            P(("dp", "seq", "head"), None),
            P(None, None, "head"),
            P("head", None),
            P(("dp", "head"), None, None),
        ),
        out_specs=P(("dp", "seq", "head"), None),
        check_vma=False,
    )
```

profile of v0, /device:TPU:6, one launch (start us, length us, event | category | flops | bytes accessed | tf_op | source)
XLA Modules:
  0.0 232.3 jit_solution(14859158136180378359)
XLA Ops:
  6.5 0.0 copy-start
  6.5 0.0 all-gather.4.cloned.1.call-start
  6.5 0.7 all-gather.4.cloned.1.call-update
  7.3 0.0 all-gather.6.cloned.1.call-start
  7.3 8.9 %copy.22 = bf16[2048,3,512]{0,2,1:T(8,128)(2,1)} copy(bf16[2048,3,512]{2,0,1:T(8,128)(2,1)} %param.5) | data formatting | bytes 12582912 | tf_op args[1]
  16.2 44.9 %all-gather.4.cloned.1.call-done = bf16[1024,2048]{1,0:T(8,128)(2,1)} async-done(((bf16[256,2048]{1,0:T(8,128)(2,1)}), bf16[1024,2048]{1,0:T(8,128)(2,1)}) %all-gather.4.cloned.1.call-update) | async-done | bytes 4194320 | tf_op jit(solution)/shard_map/all_gather | solution.py:14
  61.1 10.1 %convolution_convert_fusion = bf16[1024,1536]{1,0:T(8,128)(2,1)S(1)} fusion(bf16[1024,2048]{1,0:T(8,128)(2,1)} %all-gather.4.cloned.1.call-done, bf16[2048,1536]{0,1:T(8,128)(2,1)} %bitcast.55), kind=kOutput, calls=%fused_computation.7 | convolution fusion | flops 6444023808 | bytes 13631488 | tf_op jit(solution)/shard_map/dot_general | solution.py:13
  71.2 0.0 copy-start.1
  71.2 1.7 copy-done.1
  72.9 1.2 slice_bitcast_fusion
  74.1 1.4 copy.38
  75.4 2.7 %convolution_convert_fusion.2 = bf16[4,128,128]{2,1,0:T(8,128)(2,1)} fusion(bf16[1024,4,128]{0,2,1:T(8,128)(2,1)} %bitcast.57, bf16[128,4,8,128]{3,2,1,0:T(8,128)(2,1)} %get-tuple-element.9), kind=kOutput, calls=%fused_computation.17 | convolution fusion | flops 134283264 | bytes 2228224 | tf_op jit(solution)/shard_map/thd,the->hde/dot_general | solution.py:20
  78.1 0.0 all-gather.6.cloned.1.call-update
  78.2 0.2 reduce-scatter.2.cloned.1.call-start
  78.4 0.8 iota_compare_fusion.1
  79.2 1.2 iota_compare_fusion
  80.4 3.0 %slice_bitcast_fusion.2 = (bf16[64,4,8,128]{3,2,1,0:T(8,128)(2,1)}, bf16[64,4,8,128]{3,2,1,0:T(8,128)(2,1)}, bf16[64,4,8,128]{3,2,1,0:T(8,128)(2,1)S(1)}, bf16[512,512]{1,0:T(8,128)(2,1)S(1)}) fusion(bf16[1024,1536]{1,0:T(8,128)(2,1)} %copy-done.1), kind=kLoop, calls=%fused_computation.39 | loop fusion | bytes 4194304
  83.3 1.0 copy.37
  84.3 5.4 %fusion.1 = f32[4,128,512]{2,1,0:T(8,128)} fusion(bf16[1024,4,128]{0,2,1:T(8,128)(2,1)} %bitcast.58, pred[512,1024]{1,0:T(8,128)(4,1)} %iota_compare_fusion, bf16[128,4,8,128]{3,2,1,0:T(8,128)(2,1)} %get-tuple-element.9, bf16[64,4,8,128]{3,2,1,0:T(8,128)(2,1)} %get-tuple-element.6), kind=kOutput, calls=%fused_computation.3 | convolution fusion | flops 1077936128 | bytes 4194304 | tf_op jit(solution)/shard_map/hst,thd->shd/dot_general | solution.py:40
  89.7 0.0 copy-start.4
  89.7 72.5 %all-gather.6.cloned.1.call-done = bf16[128,128,128]{2,1,0:T(8,128)(2,1)} async-done(((bf16[4,128,128]{2,1,0:T(8,128)(2,1)}), bf16[128,128,128]{2,1,0:T(8,128)(2,1)}) %all-gather.6.cloned.1.call-update) | async-done | bytes 4194320 | tf_op jit(solution)/shard_map/all_gather | solution.py:22
  162.3 3.2 %fusion = f32[4,128,128]{2,1,0:T(8,128)S(1)} fusion(bf16[32,4,128,128]{3,2,1,0:T(8,128)(2,1)} %bitcast.56, f32[32]{0:T(128)S(1)} %compare_convert_fusion), kind=kLoop, calls=%fused_computation.1 | loop fusion | flops 6225920 | bytes 4456576 | tf_op jit(solution)/shard_map/reduce_sum | solution.py:27
  165.5 0.0 copy-done.4
  165.5 0.0 copy-start.3
  165.5 1.3 fusion.26
  166.9 3.9 %multiply_reduce_fusion.1 = (f32[512,4]{0,1:T(4,128)S(1)}, f32[512,4,128]{0,2,1:T(8,128)}) fusion(f32[4,128,512]{2,1,0:T(8,128)} %fusion.26, bf16[512,4,128]{0,2,1:T(8,128)(2,1)} %bitcast.61, pred[512,512]{1,0:T(8,128)(4,1)} %iota_compare_fusion.1, bf16[64,4,8,128]{3,2,1,0:T(8,128)(2,1)} %get-tuple-element.5, bf16[64,4,8,128]{3,2,1,0:T(8,128)(2,1)S(1)} %get-tuple-element.7), kind=kOutput, calls=%fused_computation.27 | convolution fusion | flops 539752448 | bytes 3940352 | tf_op jit(solution)/shard_map/hst,thd->shd/dot_general | solution.py:40
  170.8 0.0 copy-done.3
  170.8 1.6 multiply_reduce_fusion
  172.4 1.4 multiply_convert_fusion.1
  173.8 0.1 multiply_convert_fusion
  173.9 0.0 copy-done
  173.9 4.3 %convolution_convert_fusion.1 = bf16[1024,2048]{1,0:T(8,128)(2,1)} fusion(bf16[512,2048]{1,0:T(8,128)(2,1)S(1)} %copy-done, bf16[512,512]{0,1:T(8,128)(2,1)S(1)} %bitcast.60, bf16[512,512]{0,1:T(8,128)(2,1)S(1)} %bitcast.59), kind=kOutput, calls=%fused_computation.8 | convolution fusion | flops 2151677952 | bytes 7340032 | tf_op jit(solution)/shard_map/dot_general | solution.py:50
  178.3 0.0 copy-start.2
  178.3 0.0 reduce-scatter.2.cloned.1.call-update
  178.3 44.9 %reduce-scatter.2.cloned.1.call-done = bf16[256,2048]{1,0:T(8,128)(2,1)} async-done(((bf16[1024,2048]{1,0:T(8,128)(2,1)}), bf16[256,2048]{1,0:T(8,128)(2,1)}) %reduce-scatter.2.cloned.1.call-update) | async-done | bytes 1048592 | tf_op jit(solution)/shard_map/reduce_scatter | solution.py:49
  223.2 0.0 copy-done.2
  223.2 2.6 %add_convert_fusion = bf16[256,2048]{1,0:T(8,128)(2,1)} fusion(bf16[256,2048]{1,0:T(8,128)(2,1)} %reduce-scatter.2.cloned.1.call-done, bf16[256,2048]{1,0:T(8,128)(2,1)S(1)} %copy-done.2), kind=kLoop, calls=%fused_computation.10 | loop fusion | flops 2097152 | bytes 3145728 | tf_op jit(solution)/shard_map/convert_element_type | solution.py:55
  (5 shorter events, 0.1 us)
Async XLA Ops:
  6.5 167.4 %copy-start = (bf16[512,2048]{1,0:T(8,128)(2,1)S(1)}, bf16[512,2048]{1,0:T(8,128)(2,1)}, u32[]{:S(2)}) copy-start(bf16[512,2048]{1,0:T(8,128)(2,1)} %param.6) | copy-start | bytes 6291460
  6.5 54.6 %all-gather.4.cloned.1.call-start = ((), (), s32[]{:S(2)}) async-start(), calls=%async_computation.1 | async-start | bytes 5242880 | tf_op jit(solution)/shard_map/all_gather | solution.py:14
  7.3 155.0 %all-gather.6.cloned.1.call-start = ((), (), s32[]{:S(2)}) async-start(), calls=%async_computation.3 | async-start | bytes 4325376 | tf_op jit(solution)/shard_map/all_gather | solution.py:22
  71.2 1.7 copy-start.1
  78.2 145.0 %reduce-scatter.2.cloned.1.call-start = ((), (), s32[]{:S(2)}) async-start(), calls=%async_computation.2 | async-start | bytes 5242880 | tf_op jit(solution)/shard_map/reduce_scatter | solution.py:49
  89.7 75.8 %copy-start.4 = (f32[4,128,128]{2,1,0:T(8,128)S(1)}, f32[4,128,128]{2,1,0:T(8,128)}, u32[]{:S(2)}) copy-start(f32[4,128,128]{2,1,0:T(8,128)} %param.7) | copy-start | bytes 786436
  165.5 5.3 %copy-start.3 = (bf16[64,4,8,128]{3,2,1,0:T(8,128)(2,1)S(1)}, bf16[64,4,8,128]{3,2,1,0:T(8,128)(2,1)}, u32[]{:S(2)}) copy-start(bf16[64,4,8,128]{3,2,1,0:T(8,128)(2,1)} %get-tuple-element.6) | copy-start | bytes 1572868
  178.3 44.9 %copy-start.2 = (bf16[256,2048]{1,0:T(8,128)(2,1)S(1)}, bf16[256,2048]{1,0:T(8,128)(2,1)}, u32[]{:S(2)}) copy-start(bf16[256,2048]{1,0:T(8,128)(2,1)} %param.4) | copy-start | bytes 3145732
Sparse Core Ops, SparseCore 0:
  9.2 51.9 all-gather.3
  78.3 83.9 all-gather.5
  178.4 44.7 reduce-scatter.1
where the time goes:
time: 236 us; the launch traced here: 232 us
  waiting for transfers between devices  163 us (69%)
  matrix products  29.4 us (12%)
  local copies, waits for them, and re-layouts  17.1 us (7%)
  between operations  13.2 us (6%)
  other arithmetic  9.26 us (4%)
    all_gather x1, waiting for transfers between devices, on_device(): lax.all_gather(local_state[None].astype(jnp.bfloat16), 'seq', axis=0, til...  72.5 us
    all_gather x1, waiting for transfers between devices, on_device(): lax.all_gather(tokens, 'head', axis=0, tiled=True)  44.9 us
    reduce_scatter x1, waiting for transfers between devices, on_device(): lax.psum_scatter(jnp.dot(normed, out_weight, preferred_element_type=jnp.f...  44.9 us
    unnamed x13, local copies, waits for them, and re-layouts  14.7 us
    dot_general x1, matrix products, on_device(): jnp.dot(lax.all_gather(tokens, 'head', axis=0, tiled=True), flat, preferr...  10.1 us
    dot_general x2, matrix products, on_device(): jnp.einsum('hst,thd->shd', weights, values[:upper], preferred_element_typ...  9.34 us
  transfers between devices with their start and end apart: 3, of which 3 were waited for; matrix products, arithmetic and copies ran while one was open for 9% of the time, Pallas kernels for 0%

commit v1 on v0

v1 whole, which is shorter than its diff:
```python
import functools

import jax
import jax.numpy as jnp
from jax import lax
from jax.experimental import pallas as pl
from jax.experimental.pallas import tpu as pltpu
from jax.sharding import PartitionSpec as P

MESH = pl.DeviceIdType.MESH
F32 = jnp.float32
BF16 = jnp.bfloat16

NZ = 8
NX = 4
PIECES = 4
HALVES = 2


class Ring:
    def __init__(self, block, me, n, sgn, device, send, recv, pieces=1):
        self.block, self.me, self.n, self.sgn = block, me, n, sgn
        self.device, self.send, self.recv = device, send, recv
        self.pieces = pieces
        self.far = n // 2
        self.near = n - 1 - self.far

    def at(self, steps):
        return lax.rem(self.me + self.sgn * steps + 2 * self.n, self.n)

    def hops(self, way):
        return self.far if way > 0 else self.near

    def sem(self, way, hop, piece):
        base = 0 if way > 0 else self.far
        return (base + hop) * self.pieces + piece

    def copy(self, way, hop, piece, src, dst):
        number = self.sem(way, hop, piece)
        return pltpu.make_async_remote_copy(
            src_ref=src,
            dst_ref=dst,
            send_sem=self.send.at[number],
            recv_sem=self.recv.at[number],
            device_id=self.device(self.at(way)),
            device_id_type=MESH,
        )

    def start(self, way, hop, piece=0, src=None):
        if hop < self.hops(way):
            here = self.block(-way * hop, self.at(-way * hop), piece)
            self.copy(way, hop, piece, here if src is None else src, self.landing(way, hop, piece)).start()

    def landing(self, way, hop, piece):
        return self.block(-way * (hop + 1), self.at(-way * hop), piece)

    def arrived(self, way, hop, piece=0):
        if hop < self.hops(way):
            here = self.block(-way * (hop + 1), self.at(-way * (hop + 1)), piece)
            self.copy(way, hop, piece, here, here).wait_recv()

    def pass_on(self, way, hop, piece=0):
        self.arrived(way, hop, piece)
        self.start(way, hop + 1, piece)

    def finish(self):
        for way in (1, -1):
            for hop in range(self.hops(way)):
                for piece in range(self.pieces):
                    here = self.block(-way * hop, self.at(-way * hop), piece)
                    self.copy(way, hop, piece, here, here).wait_send()


def kernel(
    ny,
    tok_hbm,
    wq_hbm,
    wo_hbm,
    prefix_ref,
    out_ref,
    tok,
    wq,
    wo,
    qkv,
    st,
    off,
    mixed,
    nbuf,
    nrec,
    acc,
    sbuf,
    rbuf,
    pbuf,
    cbuf,
    lsem,
    tsend,
    trecv,
    xsend,
    xrecv,
    r1send,
    r1recv,
    r2send,
    r2recv,
    bsend,
    brecv,
    ssend,
    srecv,
    csend,
    crecv,
    nsend,
    nrecv,
):
    nseq = ny * NZ
    rows = tok.shape[1]
    heads = st.shape[1]
    hd = st.shape[2]
    width = wo.shape[-1]
    me = lax.axis_index("seq")
    mx = lax.axis_index("head")
    mc = lax.axis_index("dp")
    my = me // NZ
    mz = lax.rem(me, NZ)
    sgn = 1 - 2 * mc

    loads = [pltpu.make_async_copy(tok_hbm, tok.at[0], lsem.at[0])]
    for part in range(3):
        loads.append(pltpu.make_async_copy(wq_hbm.at[part], wq.at[part], lsem.at[1 + part]))
    for band in range(4):
        loads.append(
            pltpu.make_async_copy(
                wo_hbm.at[:, :, :, pl.ds(band * width, width)], wo.at[band, 0], lsem.at[4 + band]
            )
        )
    for load in loads:
        load.start()

    barrier = pltpu.get_barrier_semaphore()
    for step in range(1, NX):
        pl.semaphore_signal(
            barrier, inc=1, device_id={"head": lax.rem(mx + step, NX)}, device_id_type=MESH
        )
    pl.semaphore_signal(barrier, inc=1, device_id={"dp": 1 - mc}, device_id_type=MESH)

    def greet(step, carry):
        pl.semaphore_signal(
            barrier, inc=1, device_id={"seq": lax.rem(me + step, nseq)}, device_id_type=MESH
        )
        return carry

    lax.fori_loop(1, nseq, greet, 0)
    pl.semaphore_wait(barrier, NX - 1 + 1 + nseq - 1)

    def slice_copy(side, step):
        band = mc * 2 + side
        number = side * (NX - 1) + step - 1
        return pltpu.make_async_remote_copy(
            src_ref=wo_hbm.at[my, mz, :, pl.ds(pl.multiple_of(band * width, width), width)],
            dst_ref=wo.at[band, NX - step, my, mz],
            send_sem=xsend.at[number],
            recv_sem=xrecv.at[number],
            device_id={"head": lax.rem(mx + step, NX)},
            device_id_type=MESH,
        )

    for side in range(2):
        for step in range(1, NX):
            slice_copy(side, step).start()

    prow = rows // PIECES

    def tok_block(relative, index, piece):
        return tok.at[relative % NX, pl.ds(piece * prow, prow)]

    tring = Ring(
        tok_block, mx, NX, sgn, lambda index: {"head": index}, tsend, trecv, pieces=PIECES
    )
    for piece in range(PIECES):
        for way in (1, -1):
            tring.start(way, 0, piece, src=tok_hbm.at[pl.ds(piece * prow, prow)])

    def along_y(index):
        return {"seq": index * NZ + mz}

    def along_z(index):
        return {"seq": my * NZ + index}

    first = [
        Ring(
            lambda relative, index, piece: wo.at[mc * 2, pl.ds(1, NX - 1), index, mz],
            my, ny, sgn, along_y, r1send.at[0], r1recv.at[0],
        ),
        Ring(
            lambda relative, index, piece: wo.at[mc * 2 + 1, pl.ds(1, NX - 1), my, index],
            mz, NZ, sgn, along_z, r1send.at[1], r1recv.at[1],
        ),
    ]
    second = [
        Ring(
            lambda relative, index, piece: wo.at[mc * 2, pl.ds(1, NX - 1), :, index],
            mz, NZ, sgn, along_z, r2send.at[0], r2recv.at[0],
        ),
        Ring(
            lambda relative, index, piece: wo.at[mc * 2 + 1, pl.ds(1, NX - 1), index],
            my, ny, sgn, along_y, r2send.at[1], r2recv.at[1],
        ),
    ]

    def hop(ring, number):
        for way in (1, -1):
            ring.pass_on(way, number)

    def begin(ring):
        for way in (1, -1):
            ring.start(way, 0)

    def group_of(slot):
        return lax.rem(mx + sgn * slot + 2 * NX, NX)

    def project(slot, lower, count):
        group = group_of(slot)
        pair = wq.shape[2] // 2

        def body(step, carry):
            part = step // 2
            side = lax.rem(step, 2)
            result = jnp.dot(
                tok[slot, pl.ds(lower, count)],
                wq[part, :, pl.ds(pl.multiple_of(side * pair, pair), pair)],
                preferred_element_type=F32,
            ).astype(BF16)
            for half in range(2):
                qkv[part * heads + side * 2 + half, group, pl.ds(lower, count)] = result[
                    :, half * hd : (half + 1) * hd
                ]
            return carry

        lax.fori_loop(0, 6, body, 0)

    def state(slot):
        group = group_of(slot)
        for head in range(heads):
            st[group, head] = lax.dot_general(
                qkv[heads + head, group],
                qkv[2 * heads + head, group],
                (((0,), (0,)), ((), ())),
                preferred_element_type=F32,
            )

    def slices_in(side):
        for step in range(1, NX):
            copy = slice_copy(side, step)
            band = mc * 2 + side
            number = side * (NX - 1) + step - 1
            here = wo.at[band, NX - step, my, mz]
            pltpu.make_async_remote_copy(
                src_ref=here, dst_ref=here, send_sem=xsend.at[number], recv_sem=xrecv.at[number],
                device_id={"head": lax.rem(mx + step, NX)}, device_id_type=MESH,
            ).wait_recv()
        begin(first[side])

    for side in range(2):
        slices_in(side)
    for load in loads[:4]:
        load.wait()
    project(0, 0, rows)
    hop(first[0], 0)
    hop(first[1], 0)
    hop(first[0], 1)
    begin(second[0])
    hop(first[1], 1)
    tring.pass_on(1, 0, 0)
    hop(first[1], 2)
    hop(first[1], 3)
    begin(second[1])
    state(0)
    tring.pass_on(1, 0, 1)
    hop(second[0], 0)
    tring.pass_on(1, 0, 2)
    tring.pass_on(1, 0, 3)
    hop(second[0], 1)
    hop(second[1], 0)
    project(NX - 1, 0, rows)
    state(NX - 1)
    for piece in range(PIECES):
        tring.arrived(-1, 0, piece)
    project(1, 0, rows)
    state(1)
    hop(second[0], 2)
    hop(second[0], 3)
    hop(second[1], 1)

    def sibling(side):
        band = wo.at[mc * 2 + side, pl.ds(1, NX - 1)]
        return pltpu.make_async_remote_copy(
            src_ref=band, dst_ref=band, send_sem=bsend.at[side], recv_sem=brecv.at[side],
            device_id={"dp": 1 - mc}, device_id_type=MESH,
        )

    for side in range(2):
        sibling(side).start()

    for half in range(2):
        for piece in range(half * PIECES // 2, (half + 1) * PIECES // 2):
            tring.arrived(1, 1, piece)
        project(2, half * rows // 2, rows // 2)
    state(2)

    per_head = nseq // heads
    for head in range(heads):
        total = st[0, head] + st[1, head] + st[2, head] + st[3, head]
        sbuf[head * per_head : (head + 1) * per_head] = total.astype(BF16).reshape(
            per_head, hd // per_head, hd
        )

    def out_copy(step):
        to = lax.rem(me + step, nseq)
        return pltpu.make_async_remote_copy(
            src_ref=sbuf.at[to], dst_ref=rbuf.at[me], send_sem=ssend.at[step],
            recv_sem=srecv.at[step], device_id={"seq": to}, device_id_type=MESH,
        )

    def in_copy(step):
        here = lax.rem(me - step + nseq, nseq)
        return pltpu.make_async_remote_copy(
            src_ref=sbuf.at[here], dst_ref=rbuf.at[here], send_sem=ssend.at[step],
            recv_sem=srecv.at[step], device_id={"seq": here}, device_id_type=MESH,
        )

    def back_copy(step):
        to = lax.rem(me + step, nseq)
        return pltpu.make_async_remote_copy(
            src_ref=pbuf.at[to], dst_ref=cbuf.at[me], send_sem=csend.at[step],
            recv_sem=crecv.at[step], device_id={"seq": to}, device_id_type=MESH,
        )

    def carried_copy(step):
        here = lax.rem(me - step + nseq, nseq)
        return pltpu.make_async_remote_copy(
            src_ref=pbuf.at[here], dst_ref=cbuf.at[here], send_sem=csend.at[step],
            recv_sem=crecv.at[step], device_id={"seq": here}, device_id_type=MESH,
        )

    def each(action):
        def body(step, carry):
            action(step)
            return carry

        lax.fori_loop(1, nseq, body, 0)

    each(lambda step: out_copy(step).start())
    rbuf[me] = sbuf[me]

    for head in range(heads):
        running = st[0, head]
        off[1, head] = running.astype(BF16)
        for group in range(2, NX):
            running = running + st[group - 1, head]
            off[group, head] = running.astype(BF16)
        off[0, head] = jnp.zeros((hd, hd), BF16)

    def inner(group):
        causal = lax.broadcasted_iota(jnp.int32, (rows, rows), 0) >= lax.broadcasted_iota(
            jnp.int32, (rows, rows), 1
        )
        for head in range(heads):
            query = qkv[head, group]
            scores = lax.dot_general(
                query, qkv[heads + head, group], (((1,), (1,)), ((), ())),
                preferred_element_type=F32,
            )
            weights = jnp.where(causal, scores, 0.0).astype(BF16)
            mixed[group, head] = jnp.dot(
                weights, qkv[2 * heads + head, group], preferred_element_type=F32
            ) + jnp.dot(query, off[group, head], preferred_element_type=F32)

    def inner_body(group, carry):
        inner(group)
        return carry

    lax.fori_loop(0, 1, inner_body, 0)

    each(lambda step: in_copy(step).wait_recv())
    total = prefix_ref[me]
    for block in range(nseq):
        pbuf[block] = total.astype(BF16)
        if block < nseq - 1:
            total = total + rbuf[block].astype(F32)
    each(lambda step: back_copy(step).start())
    cbuf[me] = pbuf[me]

    lax.fori_loop(1, NX, inner_body, 0)
    each(lambda step: carried_copy(step).wait_recv())

    hrow = rows // HALVES

    def normed_copy(step, half):
        number = (step - 1) * HALVES + half
        return pltpu.make_async_remote_copy(
            src_ref=nbuf.at[step, pl.ds(half * hrow, hrow)],
            dst_ref=nrec.at[NX - step - 1, pl.ds(half * hrow, hrow)],
            send_sem=nsend.at[number],
            recv_sem=nrecv.at[number],
            device_id={"head": lax.rem(mx + step, NX)},
            device_id_type=MESH,
        )

    def normed_in(step, half):
        number = (NX - step - 1) * HALVES + half
        here = nrec.at[step - 1, pl.ds(half * hrow, hrow)]
        return pltpu.make_async_remote_copy(
            src_ref=here, dst_ref=here, send_sem=nsend.at[number], recv_sem=nrecv.at[number],
            device_id={"head": lax.rem(mx + step, NX)}, device_id_type=MESH,
        )

    def normalize(step, half):
        group = lax.rem(mx + step, NX)
        lower = half * hrow
        for head in range(heads):
            carried = cbuf[head * per_head : (head + 1) * per_head].reshape(hd, hd)
            value = mixed[group, head, pl.ds(lower, hrow)] + jnp.dot(
                qkv[head, group, pl.ds(lower, hrow)], carried, preferred_element_type=F32
            )
            factor = lax.rsqrt(jnp.mean(value * value, axis=-1, keepdims=True) + 1e-06)
            nbuf[step, pl.ds(lower, hrow), head * hd : (head + 1) * hd] = (value * factor).astype(BF16)

    for half in range(HALVES):
        for step in (2, 1, 3):
            normalize(step, half)
            normed_copy(step, half).start()
    for half in range(HALVES):
        normalize(0, half)

    for load in loads[4:]:
        load.wait()

    def weight(band, relative):
        return wo[band, relative].reshape(nseq * 16, width)

    def own(band, carry):
        columns = pl.ds(pl.multiple_of(band * width, width), width)
        acc[:, columns] = tok[0, :, columns].astype(F32) + jnp.dot(
            nbuf[0], weight(band, 0), preferred_element_type=F32
        )
        return carry

    lax.fori_loop(0, 4, own, 0)
    for side in range(2):
        band = wo.at[(1 - mc) * 2 + side, pl.ds(1, NX - 1)]
        pltpu.make_async_remote_copy(
            src_ref=band, dst_ref=band, send_sem=bsend.at[side], recv_sem=brecv.at[side],
            device_id={"dp": 1 - mc}, device_id_type=MESH,
        ).wait_recv()

    for half in range(HALVES):
        lower = half * hrow
        for place, step in enumerate((2, 1, 3)):
            normed_in(step, half).wait_recv()

            def project_out(band, carry):
                columns = pl.ds(pl.multiple_of(band * width, width), width)
                value = acc[lower : lower + hrow, columns] + jnp.dot(
                    nrec[step - 1, lower : lower + hrow], weight(band, step), preferred_element_type=F32
                )
                if place < 2:
                    acc[lower : lower + hrow, columns] = value
                else:
                    out_ref[lower : lower + hrow, columns] = value.astype(BF16)
                return carry

            lax.fori_loop(0, 4, project_out, 0)

    for side in range(2):
        for step in range(1, NX):
            slice_copy(side, step).wait_send()
        sibling(side).wait_send()
    for ring in [tring] + first + second:
        ring.finish()
    each(lambda step: out_copy(step).wait_send())
    each(lambda step: back_copy(step).wait_send())
    for step in range(1, NX):
        for half in range(HALVES):
            normed_copy(step, half).wait_send()


def on_device(tokens, qkv_weight, out_weight, prefix_state):
    rows, model_width = tokens.shape
    heads, hd, _ = prefix_state.shape
    group_width = heads * hd
    nseq = lax.axis_size("seq")
    ny = nseq // NZ
    width = model_width // 4
    slice_rows = group_width // nseq
    dma = pltpu.SemaphoreType.DMA
    return pl.pallas_call(
        functools.partial(kernel, ny),
        out_shape=jax.ShapeDtypeStruct((rows, model_width), BF16),
        in_specs=[pl.BlockSpec(memory_space=pl.ANY)] * 3 + [pl.BlockSpec(memory_space=pltpu.VMEM)],
        out_specs=pl.BlockSpec(memory_space=pltpu.VMEM),
        scratch_shapes=[
            pltpu.VMEM((NX, rows, model_width), BF16),
            pltpu.VMEM((3, model_width, group_width), BF16),
            pltpu.VMEM((4, NX, ny, NZ, slice_rows, width), BF16),
            pltpu.VMEM((3 * heads, NX, rows, hd), BF16),
            pltpu.VMEM((NX, heads, hd, hd), F32),
            pltpu.VMEM((NX, heads, hd, hd), BF16),
            pltpu.VMEM((NX, heads, rows, hd), F32),
            pltpu.VMEM((NX, rows, group_width), BF16),
            pltpu.VMEM((NX - 1, rows, group_width), BF16),
            pltpu.VMEM((rows, model_width), F32),
            pltpu.VMEM((nseq, slice_rows, hd), BF16),
            pltpu.VMEM((nseq, slice_rows, hd), BF16),
            pltpu.VMEM((nseq, slice_rows, hd), BF16),
            pltpu.VMEM((nseq, slice_rows, hd), BF16),
            dma((8,)),
            dma((3 * PIECES,)),
            dma((3 * PIECES,)),
            dma((2 * (NX - 1),)),
            dma((2 * (NX - 1),)),
            dma((2, NZ)),
            dma((2, NZ)),
            dma((2, NZ)),
            dma((2, NZ)),
            dma((2,)),
            dma((2,)),
            dma((nseq,)),
            dma((nseq,)),
            dma((nseq,)),
            dma((nseq,)),
            dma(((NX - 1) * HALVES,)),
            dma(((NX - 1) * HALVES,)),
        ],
        compiler_params=pltpu.CompilerParams(
            collective_id=0, has_side_effects=True, vmem_limit_bytes=56 * 1024 * 1024
        ),
        name="layer",
    )(
        tokens,
        jnp.transpose(qkv_weight, (1, 0, 2)),
        out_weight.reshape(ny, NZ, slice_rows, model_width),
        prefix_state.reshape(nseq, slice_rows, hd),
    )


def solution(mesh):
    return jax.shard_map(
        on_device,
        mesh=mesh,
        in_specs=(
            P(("dp", "seq", "head"), None),
            P(None, None, "head"),
            P("head", None),
            P(("dp", "head"), None, None),
        ),
        out_specs=P(("dp", "seq", "head"), None),
        check_vma=False,
    )
```

time: 236 us -> 86.2 us (0.37); the launches traced: 232 us -> 86 us
  waiting for transfers between devices: 163 us -> 0 us
  Pallas kernels: 0 us -> 83.7 us
  matrix products: 29.4 us -> 0 us
  local copies, waits for them, and re-layouts: 17.1 us -> 2.3 us
  between operations: 13.2 us -> 0.01 us
  other arithmetic: 9.26 us -> 0 us
    all_gather x2 -> x0, waiting for transfers between devices: 117 us -> none  [the longest x1 72.5 us: on_device(): lax.all_gather(local_state[None].astype(jnp.bfloat16), 'seq', axis=0, til...]
    pallas_call x0 -> x1, Pallas kernels: none -> 83.7 us  [on_device(): pl.pallas_call(functools.partial(kernel, ny), out_shape=jax.ShapeDtypeStr...]
    reduce_scatter x1 -> x0, waiting for transfers between devices: 44.9 us -> none  [on_device(): lax.psum_scatter(jnp.dot(normed, out_weight, preferred_element_type=jnp.f...]
    dot_general x7 -> x0, matrix products: 29.4 us -> none  [the longest x1 10.1 us: on_device(): jnp.dot(lax.all_gather(tokens, 'head', axis=0, tiled=True), flat, preferr...]
    unnamed x13 -> x1, local copies, waits for them, and re-layouts: 14.7 us -> 2.3 us
    convert_element_type x5 -> x0, other arithmetic: 4.1 us -> none  [the longest x1 2.58 us: on_device(): return (tokens.astype(jnp.float32) + summed).astype(jnp.bfloat16)]
    reduce_sum x1 -> x0, other arithmetic: 3.21 us -> none  [on_device(): carried = prefix_state + jnp.sum(piece * keep[:, None, None, None], axis=0)]
  transfers between devices with their start and end apart: 3 -> 0, of which waited for: 3 -> 0; matrix products, arithmetic and copies ran while one was open for 9% -> 0% of each run, Pallas kernels for 0% -> 0%
where the time goes in v1:
time: 86.2 us; the launch traced here: 86 us
  Pallas kernels  83.7 us (97%)
  local copies, waits for them, and re-layouts  2.3 us (3%)
    pallas_call x1, Pallas kernels, on_device(): pl.pallas_call(functools.partial(kernel, ny), out_shape=jax.ShapeDtypeStr...  83.7 us
    unnamed x1, local copies, waits for them, and re-layouts  2.3 us

profile of v1, /device:TPU:6, one launch (start us, length us, event | category | flops | bytes accessed | tf_op | source)
XLA Modules:
  0.0 86.0 jit_solution(15073591809188301009)
XLA Ops:
  0.0 83.7 %layer.1 = bf16[256,2048]{1,0:T(8,128)(2,1)} custom-call(bf16[256,2048]{1,0:T(8,128)(2,1)} %tok_hbm.1, bf16[3,2048,512]{2,1,0:T(8,128)(2,1)} %bitcast.3, bf16[4,8,16,2048]{3,2,1,0:T(8,128)(2,1)} %bitcast.4, f32[32,16,128]{2,1,0:T(8,128)} %bitcast.5), custom_call_target="tpu_custom_call" | custom-call | tf_op jit(solution)/shard_map/layer/pallas_call | solution.py:494
  83.7 2.3 %copy.6 = bf16[256,2048]{1,0:T(8,128)(2,1)} copy(bf16[256,2048]{1,0:T(8,128)(2,1)} %layer.1) | data formatting | bytes 2097152

commit v2 on v1

--- a/solution.py
+++ b/solution.py
@@ -76,8 +76,8 @@
     tok_hbm,
     wq_hbm,
     wo_hbm,
-    prefix_ref,
-    out_ref,
+    prefix_hbm,
+    out_hbm,
     tok,
     wq,
     wo,
@@ -92,7 +92,10 @@
     rbuf,
     pbuf,
     cbuf,
+    prefix,
+    out,
     lsem,
+    osem,
     tsend,
     trecv,
     xsend,
@@ -122,6 +125,21 @@
     mz = lax.rem(me, NZ)
     sgn = 1 - 2 * mc
 
+    barrier = pltpu.get_barrier_semaphore()
+    for step in range(1, NX):
+        pl.semaphore_signal(
+            barrier, inc=1, device_id={"head": lax.rem(mx + step, NX)}, device_id_type=MESH
+        )
+    pl.semaphore_signal(barrier, inc=1, device_id={"dp": 1 - mc}, device_id_type=MESH)
+
+    for step in (1, NZ - 1):
+        pl.semaphore_signal(
+            barrier, inc=1, device_id={"seq": my * NZ + lax.rem(mz + step, NZ)}, device_id_type=MESH
+        )
+    for step in (1, ny - 1):
+        pl.semaphore_signal(
+            barrier, inc=1, device_id={"seq": lax.rem(my + step, ny) * NZ + mz}, device_id_type=MESH
+        )
     loads = [pltpu.make_async_copy(tok_hbm, tok.at[0], lsem.at[0])]
     for part in range(3):
         loads.append(pltpu.make_async_copy(wq_hbm.at[part], wq.at[part], lsem.at[1 + part]))
@@ -131,24 +149,11 @@
                 wo_hbm.at[:, :, :, pl.ds(band * width, width)], wo.at[band, 0], lsem.at[4 + band]
             )
         )
+    loads.append(pltpu.make_async_copy(prefix_hbm.at[me], prefix, lsem.at[8]))
     for load in loads:
         load.start()
 
-    barrier = pltpu.get_barrier_semaphore()
-    for step in range(1, NX):
-        pl.semaphore_signal(
-            barrier, inc=1, device_id={"head": lax.rem(mx + step, NX)}, device_id_type=MESH
-        )
-    pl.semaphore_signal(barrier, inc=1, device_id={"dp": 1 - mc}, device_id_type=MESH)
-
-    def greet(step, carry):
-        pl.semaphore_signal(
-            barrier, inc=1, device_id={"seq": lax.rem(me + step, nseq)}, device_id_type=MESH
-        )
-        return carry
-
-    lax.fori_loop(1, nseq, greet, 0)
-    pl.semaphore_wait(barrier, NX - 1 + 1 + nseq - 1)
+    pl.semaphore_wait(barrier, NX - 1 + 1 + 4)
 
     def slice_copy(side, step):
         band = mc * 2 + side
@@ -168,15 +173,37 @@
 
     prow = rows // PIECES
 
-    def tok_block(relative, index, piece):
-        return tok.at[relative % NX, pl.ds(piece * prow, prow)]
-
-    tring = Ring(
-        tok_block, mx, NX, sgn, lambda index: {"head": index}, tsend, trecv, pieces=PIECES
-    )
-    for piece in range(PIECES):
-        for way in (1, -1):
-            tring.start(way, 0, piece, src=tok_hbm.at[pl.ds(piece * prow, prow)])
+    loads[0].wait()
+
+    def tok_copy(way, hop, piece, slot, landing):
+        number = ((0 if way > 0 else 1) + 2 * hop) * PIECES + piece
+        lower = piece * prow
+        return pltpu.make_async_remote_copy(
+            src_ref=tok.at[slot, pl.ds(lower, prow)],
+            dst_ref=tok.at[landing, pl.ds(lower, prow)],
+            send_sem=tsend.at[number],
+            recv_sem=trecv.at[number],
+            device_id={"head": lax.rem(mx + way + NX, NX)},
+            device_id_type=MESH,
+        )
+
+    side_of = {1: NX - 1, -1: 1}
+    middle = PIECES // 2
+    passed = {1: range(middle), -1: range(middle, PIECES)}
+
+    def tok_start(way, hop, piece):
+        if hop == 0:
+            tok_copy(way, 0, piece, 0, side_of[way]).start()
+        else:
+            tok_copy(way, 1, piece, side_of[way], 2).start()
+
+    def tok_arrived(way, hop, piece):
+        here = side_of[way] if hop == 0 else 2
+        tok_copy(way, hop, piece, here, here).wait_recv()
+
+    for step in range(PIECES):
+        tok_start(1, 0, step)
+        tok_start(-1, 0, (step + middle) % PIECES)
 
     def along_y(index):
         return {"seq": index * NZ + mz}
@@ -214,9 +241,9 @@
             ring.start(way, 0)
 
     def group_of(slot):
-        return lax.rem(mx + sgn * slot + 2 * NX, NX)
-
-    def project(slot, lower, count):
+        return lax.rem(mx + slot, NX)
+
+    def project(slot, first_part=0, parts=3, lower=0, count=rows):
         group = group_of(slot)
         pair = wq.shape[2] // 2
 
@@ -234,7 +261,7 @@
                 ]
             return carry
 
-        lax.fori_loop(0, 6, body, 0)
+        lax.fori_loop(2 * first_part, 2 * (first_part + parts), body, 0)
 
     def state(slot):
         group = group_of(slot)
@@ -248,7 +275,6 @@
 
     def slices_in(side):
         for step in range(1, NX):
-            copy = slice_copy(side, step)
             band = mc * 2 + side
             number = side * (NX - 1) + step - 1
             here = wo.at[band, NX - step, my, mz]
@@ -260,34 +286,32 @@
 
     for side in range(2):
         slices_in(side)
-    for load in loads[:4]:
+    for load in loads[1:4]:
         load.wait()
-    project(0, 0, rows)
+    project(0)
     hop(first[0], 0)
     hop(first[1], 0)
     hop(first[0], 1)
     begin(second[0])
     hop(first[1], 1)
-    tring.pass_on(1, 0, 0)
     hop(first[1], 2)
+    state(0)
     hop(first[1], 3)
     begin(second[1])
-    state(0)
-    tring.pass_on(1, 0, 1)
     hop(second[0], 0)
-    tring.pass_on(1, 0, 2)
-    tring.pass_on(1, 0, 3)
+    for step in range(middle):
+        for way in (1, -1):
+            piece = passed[way][step]
+            tok_arrived(way, 0, piece)
+            tok_start(way, 1, piece)
     hop(second[0], 1)
     hop(second[1], 0)
-    project(NX - 1, 0, rows)
-    state(NX - 1)
-    for piece in range(PIECES):
-        tring.arrived(-1, 0, piece)
-    project(1, 0, rows)
-    state(1)
+    for way in (1, -1):
+        for piece in passed[-way]:
+            tok_arrived(way, 0, piece)
+        project(side_of[way])
+        state(side_of[way])
     hop(second[0], 2)
-    hop(second[0], 3)
-    hop(second[1], 1)
 
     def sibling(side):
         band = wo.at[mc * 2 + side, pl.ds(1, NX - 1)]
@@ -296,13 +320,10 @@
             device_id={"dp": 1 - mc}, device_id_type=MESH,
         )
 
-    for side in range(2):
-        sibling(side).start()
-
-    for half in range(2):
-        for piece in range(half * PIECES // 2, (half + 1) * PIECES // 2):
-            tring.arrived(1, 1, piece)
-        project(2, half * rows // 2, rows // 2)
+    for way in (1, -1):
+        for piece in passed[way]:
+            tok_arrived(way, 1, piece)
+    project(2, 1, 2)
     state(2)
 
     per_head = nseq // heads
@@ -347,8 +368,17 @@
 
         lax.fori_loop(1, nseq, body, 0)
 
-    each(lambda step: out_copy(step).start())
+    def hops_to(step):
+        around_z, around_y = step % NZ, step // NZ
+        return min(around_z, NZ - around_z) + min(around_y, ny - around_y)
+
+    def far_first(action):
+        for step in sorted(range(1, nseq), key=hops_to, reverse=True):
+            action(step)
+
+    far_first(lambda step: out_copy(step).start())
     rbuf[me] = sbuf[me]
+    project(2, 0, 1)
 
     for head in range(heads):
         running = st[0, head]
@@ -380,13 +410,18 @@
     lax.fori_loop(0, 1, inner_body, 0)
 
     each(lambda step: in_copy(step).wait_recv())
-    total = prefix_ref[me]
+    loads[8].wait()
+    total = prefix[...]
     for block in range(nseq):
         pbuf[block] = total.astype(BF16)
         if block < nseq - 1:
             total = total + rbuf[block].astype(F32)
-    each(lambda step: back_copy(step).start())
+    far_first(lambda step: back_copy(step).start())
     cbuf[me] = pbuf[me]
+    hop(second[0], 3)
+    hop(second[1], 1)
+    for side in range(2):
+        sibling(side).start()
 
     lax.fori_loop(1, NX, inner_body, 0)
     each(lambda step: carried_copy(step).wait_recv())
@@ -430,7 +465,7 @@
     for half in range(HALVES):
         normalize(0, half)
 
-    for load in loads[4:]:
+    for load in loads[4:8]:
         load.wait()
 
     def weight(band, relative):
@@ -450,6 +485,10 @@
             src_ref=band, dst_ref=band, send_sem=bsend.at[side], recv_sem=brecv.at[side],
             device_id={"dp": 1 - mc}, device_id_type=MESH,
         ).wait_recv()
+
+    def out_store(half):
+        part = pl.ds(half * hrow, hrow)
+        return pltpu.make_async_copy(out.at[part], out_hbm.at[part], osem.at[half])
 
     for half in range(HALVES):
         lower = half * hrow
@@ -464,17 +503,25 @@
                 if place < 2:
                     acc[lower : lower + hrow, columns] = value
                 else:
-                    out_ref[lower : lower + hrow, columns] = value.astype(BF16)
+                    out[lower : lower + hrow, columns] = value.astype(BF16)
                 return carry
 
             lax.fori_loop(0, 4, project_out, 0)
-
+        out_store(half).start()
+
+    for half in range(HALVES):
+        out_store(half).wait()
     for side in range(2):
         for step in range(1, NX):
             slice_copy(side, step).wait_send()
         sibling(side).wait_send()
-    for ring in [tring] + first + second:
+    for ring in first + second:
         ring.finish()
+    for way in (1, -1):
+        for piece in range(PIECES):
+            tok_copy(way, 0, piece, 0, side_of[way]).wait_send()
+        for piece in passed[way]:
+            tok_copy(way, 1, piece, side_of[way], 2).wait_send()
     each(lambda step: out_copy(step).wait_send())
     each(lambda step: back_copy(step).wait_send())
     for step in range(1, NX):
@@ -494,8 +541,8 @@
     return pl.pallas_call(
         functools.partial(kernel, ny),
         out_shape=jax.ShapeDtypeStruct((rows, model_width), BF16),
-        in_specs=[pl.BlockSpec(memory_space=pl.ANY)] * 3 + [pl.BlockSpec(memory_space=pltpu.VMEM)],
-        out_specs=pl.BlockSpec(memory_space=pltpu.VMEM),
+        in_specs=[pl.BlockSpec(memory_space=pl.ANY)] * 4,
+        out_specs=pl.BlockSpec(memory_space=pl.ANY),
         scratch_shapes=[
             pltpu.VMEM((NX, rows, model_width), BF16),
             pltpu.VMEM((3, model_width, group_width), BF16),
@@ -511,9 +558,12 @@
             pltpu.VMEM((nseq, slice_rows, hd), BF16),
             pltpu.VMEM((nseq, slice_rows, hd), BF16),
             pltpu.VMEM((nseq, slice_rows, hd), BF16),
-            dma((8,)),
-            dma((3 * PIECES,)),
-            dma((3 * PIECES,)),
+            pltpu.VMEM((slice_rows, hd), F32),
+            pltpu.VMEM((rows, model_width), BF16),
+            dma((9,)),
+            dma((HALVES,)),
+            dma((4 * PIECES,)),
+            dma((4 * PIECES,)),
             dma((2 * (NX - 1),)),
             dma((2 * (NX - 1),)),
             dma((2, NZ)),

time: 86.2 us -> 77.9 us (0.904)
  Pallas kernels: 83.7 us -> 75.2 us
    pallas_call x1, Pallas kernels: 83.7 us -> 75.2 us  [on_device(): pl.pallas_call(functools.partial(kernel, ny), out_shape=jax.ShapeDtypeStr...]
where the time goes in v2:
time: 77.9 us; the launch traced here: 77.5 us
  Pallas kernels  75.2 us (97%)
  local copies, waits for them, and re-layouts  2.3 us (3%)
    pallas_call x1, Pallas kernels, on_device(): pl.pallas_call(functools.partial(kernel, ny), out_shape=jax.ShapeDtypeStr...  75.2 us
    unnamed x1, local copies, waits for them, and re-layouts  2.3 us

profile of v2, /device:TPU:6, one launch (start us, length us, event | category | flops | bytes accessed | tf_op | source)
XLA Modules:
  0.0 77.5 jit_solution(16282099408089949495)
XLA Ops:
  0.0 75.2 %layer.1 = bf16[256,2048]{1,0:T(8,128)(2,1)} custom-call(bf16[256,2048]{1,0:T(8,128)(2,1)} %tok_hbm.1, bf16[3,2048,512]{2,1,0:T(8,128)(2,1)} %bitcast.3, bf16[4,8,16,2048]{3,2,1,0:T(8,128)(2,1)} %bitcast.4, f32[32,16,128]{2,1,0:T(8,128)} %bitcast.5), custom_call_target="tpu_custom_call" | custom-call | tf_op jit(solution)/shard_map/layer/pallas_call | solution.py:541
  75.2 2.3 %copy.6 = bf16[256,2048]{1,0:T(8,128)(2,1)} copy(bf16[256,2048]{1,0:T(8,128)(2,1)} %layer.1) | data formatting | bytes 2097152

commit v3 on v2

--- a/solution.py
+++ b/solution.py
@@ -77,7 +77,7 @@
     wq_hbm,
     wo_hbm,
     prefix_hbm,
-    out_hbm,
+    out_ref,
     tok,
     wq,
     wo,
@@ -93,9 +93,7 @@
     pbuf,
     cbuf,
     prefix,
-    out,
     lsem,
-    osem,
     tsend,
     trecv,
     xsend,
@@ -304,12 +302,13 @@
             piece = passed[way][step]
             tok_arrived(way, 0, piece)
             tok_start(way, 1, piece)
-    hop(second[0], 1)
-    hop(second[1], 0)
     for way in (1, -1):
         for piece in passed[-way]:
             tok_arrived(way, 0, piece)
         project(side_of[way])
+        if way > 0:
+            hop(second[0], 1)
+            hop(second[1], 0)
         state(side_of[way])
     hop(second[0], 2)
 
@@ -336,37 +335,26 @@
     def out_copy(step):
         to = lax.rem(me + step, nseq)
         return pltpu.make_async_remote_copy(
-            src_ref=sbuf.at[to], dst_ref=rbuf.at[me], send_sem=ssend.at[step],
-            recv_sem=srecv.at[step], device_id={"seq": to}, device_id_type=MESH,
-        )
-
-    def in_copy(step):
-        here = lax.rem(me - step + nseq, nseq)
-        return pltpu.make_async_remote_copy(
-            src_ref=sbuf.at[here], dst_ref=rbuf.at[here], send_sem=ssend.at[step],
-            recv_sem=srecv.at[step], device_id={"seq": here}, device_id_type=MESH,
+            src_ref=sbuf.at[to], dst_ref=rbuf.at[me], send_sem=ssend.at[0],
+            recv_sem=srecv.at[0], device_id={"seq": to}, device_id_type=MESH,
         )
 
     def back_copy(step):
         to = lax.rem(me + step, nseq)
         return pltpu.make_async_remote_copy(
-            src_ref=pbuf.at[to], dst_ref=cbuf.at[me], send_sem=csend.at[step],
-            recv_sem=crecv.at[step], device_id={"seq": to}, device_id_type=MESH,
-        )
-
-    def carried_copy(step):
-        here = lax.rem(me - step + nseq, nseq)
-        return pltpu.make_async_remote_copy(
-            src_ref=pbuf.at[here], dst_ref=cbuf.at[here], send_sem=csend.at[step],
-            recv_sem=crecv.at[step], device_id={"seq": here}, device_id_type=MESH,
-        )
-
-    def each(action):
-        def body(step, carry):
-            action(step)
-            return carry
-
-        lax.fori_loop(1, nseq, body, 0)
+            src_ref=pbuf.at[to], dst_ref=cbuf.at[me], send_sem=csend.at[0],
+            recv_sem=crecv.at[0], device_id={"seq": to}, device_id_type=MESH,
+        )
+
+    def all_of(source, target, send, recv):
+        others = pl.ds(0, nseq - 1)
+        return pltpu.make_async_remote_copy(
+            src_ref=source.at[others], dst_ref=target.at[others], send_sem=send.at[0],
+            recv_sem=recv.at[0], device_id={"seq": lax.rem(me + 1, nseq)}, device_id_type=MESH,
+        )
+
+    scattered = all_of(sbuf, rbuf, ssend, srecv)
+    returned = all_of(pbuf, cbuf, csend, crecv)
 
     def hops_to(step):
         around_z, around_y = step % NZ, step // NZ
@@ -409,7 +397,7 @@
 
     lax.fori_loop(0, 1, inner_body, 0)
 
-    each(lambda step: in_copy(step).wait_recv())
+    scattered.wait_recv()
     loads[8].wait()
     total = prefix[...]
     for block in range(nseq):
@@ -424,7 +412,7 @@
         sibling(side).start()
 
     lax.fori_loop(1, NX, inner_body, 0)
-    each(lambda step: carried_copy(step).wait_recv())
+    returned.wait_recv()
 
     hrow = rows // HALVES
 
@@ -486,10 +474,6 @@
             device_id={"dp": 1 - mc}, device_id_type=MESH,
         ).wait_recv()
 
-    def out_store(half):
-        part = pl.ds(half * hrow, hrow)
-        return pltpu.make_async_copy(out.at[part], out_hbm.at[part], osem.at[half])
-
     for half in range(HALVES):
         lower = half * hrow
         for place, step in enumerate((2, 1, 3)):
@@ -503,14 +487,11 @@
                 if place < 2:
                     acc[lower : lower + hrow, columns] = value
                 else:
-                    out[lower : lower + hrow, columns] = value.astype(BF16)
+                    out_ref[pl.ds(lower, hrow), columns] = value.astype(BF16)
                 return carry
 
             lax.fori_loop(0, 4, project_out, 0)
-        out_store(half).start()
-
-    for half in range(HALVES):
-        out_store(half).wait()
+
     for side in range(2):
         for step in range(1, NX):
             slice_copy(side, step).wait_send()
@@ -522,8 +503,8 @@
             tok_copy(way, 0, piece, 0, side_of[way]).wait_send()
         for piece in passed[way]:
             tok_copy(way, 1, piece, side_of[way], 2).wait_send()
-    each(lambda step: out_copy(step).wait_send())
-    each(lambda step: back_copy(step).wait_send())
+    scattered.wait_send()
+    returned.wait_send()
     for step in range(1, NX):
         for half in range(HALVES):
             normed_copy(step, half).wait_send()
@@ -542,7 +523,7 @@
         functools.partial(kernel, ny),
         out_shape=jax.ShapeDtypeStruct((rows, model_width), BF16),
         in_specs=[pl.BlockSpec(memory_space=pl.ANY)] * 4,
-        out_specs=pl.BlockSpec(memory_space=pl.ANY),
+        out_specs=pl.BlockSpec(memory_space=pltpu.VMEM),
         scratch_shapes=[
             pltpu.VMEM((NX, rows, model_width), BF16),
             pltpu.VMEM((3, model_width, group_width), BF16),
@@ -559,9 +540,7 @@
             pltpu.VMEM((nseq, slice_rows, hd), BF16),
             pltpu.VMEM((nseq, slice_rows, hd), BF16),
             pltpu.VMEM((slice_rows, hd), F32),
-            pltpu.VMEM((rows, model_width), BF16),
             dma((9,)),
-            dma((HALVES,)),
             dma((4 * PIECES,)),
             dma((4 * PIECES,)),
             dma((2 * (NX - 1),)),
@@ -572,22 +551,27 @@
             dma((2, NZ)),
             dma((2,)),
             dma((2,)),
-            dma((nseq,)),
-            dma((nseq,)),
-            dma((nseq,)),
-            dma((nseq,)),
+            dma((1,)),
+            dma((1,)),
+            dma((1,)),
+            dma((1,)),
             dma(((NX - 1) * HALVES,)),
             dma(((NX - 1) * HALVES,)),
         ],
         compiler_params=pltpu.CompilerParams(
-            collective_id=0, has_side_effects=True, vmem_limit_bytes=56 * 1024 * 1024
+            collective_id=0, has_side_effects=True, vmem_limit_bytes=34 * 1024 * 1024
         ),
         name="layer",
     )(
-        tokens,
-        jnp.transpose(qkv_weight, (1, 0, 2)),
-        out_weight.reshape(ny, NZ, slice_rows, model_width),
-        prefix_state.reshape(nseq, slice_rows, hd),
+        *(
+            pltpu.with_memory_space_constraint(operand, pltpu.HBM)
+            for operand in (
+                tokens,
+                jnp.transpose(qkv_weight, (1, 0, 2)),
+                out_weight.reshape(ny, NZ, slice_rows, model_width),
+                prefix_state.reshape(nseq, slice_rows, hd),
+            )
+        )
     )
 
 

time: 77.9 us -> 74 us (0.950)
  Pallas kernels: 75.2 us -> 72.8 us
  local copies, waits for them, and re-layouts: 2.3 us -> 0.97 us
    pallas_call x1, Pallas kernels: 75.2 us -> 72.8 us  [on_device(): pl.pallas_call(functools.partial(kernel, ny), out_shape=jax.ShapeDtypeStr...]
    unnamed x1, local copies, waits for them, and re-layouts: 2.3 us -> 0.97 us
where the time goes in v3:
time: 74 us; the launch traced here: 73.8 us
  Pallas kernels  72.8 us (98%)
  local copies, waits for them, and re-layouts  0.97 us (1%)
    pallas_call x1, Pallas kernels, on_device(): pl.pallas_call(functools.partial(kernel, ny), out_shape=jax.ShapeDtypeStr...  72.8 us

profile of v3, /device:TPU:6, one launch (start us, length us, event | category | flops | bytes accessed | tf_op | source)
XLA Modules:
  0.0 73.8 jit_solution(118123273315827511)
XLA Ops:
  0.0 72.8 %layer.1 = bf16[256,2048]{1,0:T(8,128)(2,1)S(1)} custom-call(bf16[256,2048]{1,0:T(8,128)(2,1)} %tok_hbm.1, bf16[3,2048,512]{2,1,0:T(8,128)(2,1)} %bitcast.3, bf16[4,8,16,2048]{3,2,1,0:T(8,128)(2,1)} %bitcast.4, f32[32,16,128]{2,1,0:T(8,128)} %bitcast.5), custom_call_target="tpu_custom_call" | custom-call | tf_op jit(solution)/shard_map/layer/pallas_call | solution.py:522
  72.8 1.0 %copy.6 = bf16[256,2048]{1,0:T(8,128)(2,1)} copy(bf16[256,2048]{1,0:T(8,128)(2,1)S(1)} %layer.1) | data formatting | bytes 2097152

commit v4 on v3

--- a/solution.py
+++ b/solution.py
@@ -171,8 +171,6 @@
 
     prow = rows // PIECES
 
-    loads[0].wait()
-
     def tok_copy(way, hop, piece, slot, landing):
         number = ((0 if way > 0 else 1) + 2 * hop) * PIECES + piece
         lower = piece * prow
@@ -191,7 +189,15 @@
 
     def tok_start(way, hop, piece):
         if hop == 0:
-            tok_copy(way, 0, piece, 0, side_of[way]).start()
+            number = (0 if way > 0 else 1) * PIECES + piece
+            pltpu.make_async_remote_copy(
+                src_ref=tok_hbm.at[pl.ds(piece * prow, prow)],
+                dst_ref=tok.at[side_of[way], pl.ds(piece * prow, prow)],
+                send_sem=tsend.at[number],
+                recv_sem=trecv.at[number],
+                device_id={"head": lax.rem(mx + way + NX, NX)},
+                device_id_type=MESH,
+            ).start()
         else:
             tok_copy(way, 1, piece, side_of[way], 2).start()
 
@@ -230,13 +236,26 @@
         ),
     ]
 
+    def to_sibling(ring, relative):
+        side = second.index(ring)
+        block = ring.block(relative, ring.at(relative), 0)
+        pltpu.make_async_remote_copy(
+            src_ref=block, dst_ref=block, send_sem=bsend.at[side], recv_sem=brecv.at[side],
+            device_id={"dp": 1 - mc}, device_id_type=MESH,
+        ).start()
+
     def hop(ring, number):
         for way in (1, -1):
             ring.pass_on(way, number)
+        for way in (1, -1):
+            if ring in second and number < ring.hops(way):
+                to_sibling(ring, -way * (number + 1))
 
     def begin(ring):
         for way in (1, -1):
             ring.start(way, 0)
+        if ring in second:
+            to_sibling(ring, 0)
 
     def group_of(slot):
         return lax.rem(mx + slot, NX)
@@ -259,7 +278,7 @@
                 ]
             return carry
 
-        lax.fori_loop(2 * first_part, 2 * (first_part + parts), body, 0)
+        lax.fori_loop(2 * first_part, 2 * (first_part + parts), body, 0, unroll=parts == 2)
 
     def state(slot):
         group = group_of(slot)
@@ -284,7 +303,7 @@
 
     for side in range(2):
         slices_in(side)
-    for load in loads[1:4]:
+    for load in loads[:4]:
         load.wait()
     project(0)
     hop(first[0], 0)
@@ -408,8 +427,6 @@
     cbuf[me] = pbuf[me]
     hop(second[0], 3)
     hop(second[1], 1)
-    for side in range(2):
-        sibling(side).start()
 
     lax.fori_loop(1, NX, inner_body, 0)
     returned.wait_recv()
@@ -466,7 +483,7 @@
         )
         return carry
 
-    lax.fori_loop(0, 4, own, 0)
+    lax.fori_loop(0, 4, own, 0, unroll=True)
     for side in range(2):
         band = wo.at[(1 - mc) * 2 + side, pl.ds(1, NX - 1)]
         pltpu.make_async_remote_copy(
@@ -490,7 +507,7 @@
                     out_ref[pl.ds(lower, hrow), columns] = value.astype(BF16)
                 return carry
 
-            lax.fori_loop(0, 4, project_out, 0)
+            lax.fori_loop(0, 4, project_out, 0, unroll=True)
 
     for side in range(2):
         for step in range(1, NX):

time: 74 us -> 72.3 us (0.977)
  Pallas kernels: 72.8 us -> 71.3 us
    pallas_call x1, Pallas kernels: 72.8 us -> 71.3 us  [on_device(): pl.pallas_call(functools.partial(kernel, ny), out_shape=jax.ShapeDtypeStr...]
where the time goes in v4:
time: 72.3 us
  Pallas kernels  71.3 us (99%)
  local copies, waits for them, and re-layouts  0.97 us (1%)
    pallas_call x1, Pallas kernels, on_device(): pl.pallas_call(functools.partial(kernel, ny), out_shape=jax.ShapeDtypeStr...  71.3 us

profile of v4, /device:TPU:6, one launch (start us, length us, event | category | flops | bytes accessed | tf_op | source)
XLA Modules:
  0.0 72.3 jit_solution(4065693270550763597)
XLA Ops:
  0.0 71.3 %layer.1 = bf16[256,2048]{1,0:T(8,128)(2,1)S(1)} custom-call(bf16[256,2048]{1,0:T(8,128)(2,1)} %tok_hbm.1, bf16[3,2048,512]{2,1,0:T(8,128)(2,1)} %bitcast.3, bf16[4,8,16,2048]{3,2,1,0:T(8,128)(2,1)} %bitcast.4, f32[32,16,128]{2,1,0:T(8,128)} %bitcast.5), custom_call_target="tpu_custom_call" | custom-call | tf_op jit(solution)/shard_map/layer/pallas_call | solution.py:539
  71.3 1.0 %copy.6 = bf16[256,2048]{1,0:T(8,128)(2,1)} copy(bf16[256,2048]{1,0:T(8,128)(2,1)S(1)} %layer.1) | data formatting | bytes 2097152

commit v5 on v4

--- a/solution.py
+++ b/solution.py
@@ -185,7 +185,7 @@
 
     side_of = {1: NX - 1, -1: 1}
     middle = PIECES // 2
-    passed = {1: range(middle), -1: range(middle, PIECES)}
+    passed = {1: range(0, PIECES, 2), -1: range(1, PIECES, 2)}
 
     def tok_start(way, hop, piece):
         if hop == 0:
@@ -206,8 +206,8 @@
         tok_copy(way, hop, piece, here, here).wait_recv()
 
     for step in range(PIECES):
-        tok_start(1, 0, step)
-        tok_start(-1, 0, (step + middle) % PIECES)
+        for way in (1, -1):
+            tok_start(way, 0, (*passed[way], *passed[-way])[step])
 
     def along_y(index):
         return {"seq": index * NZ + mz}
@@ -338,10 +338,10 @@
             device_id={"dp": 1 - mc}, device_id_type=MESH,
         )
 
-    for way in (1, -1):
-        for piece in passed[way]:
-            tok_arrived(way, 1, piece)
-    project(2, 1, 2)
+    for wave in range(middle):
+        for way in (1, -1):
+            tok_arrived(way, 1, passed[way][wave])
+        project(2, 1, 2, wave * 2 * prow, 2 * prow)
     state(2)
 
     per_head = nseq // heads
@@ -421,9 +421,16 @@
     total = prefix[...]
     for block in range(nseq):
         pbuf[block] = total.astype(BF16)
+
+        @pl.when(block != me)
+        def _():
+            pltpu.make_async_remote_copy(
+                src_ref=pbuf.at[block], dst_ref=cbuf.at[me], send_sem=csend.at[0],
+                recv_sem=crecv.at[0], device_id={"seq": block}, device_id_type=MESH,
+            ).start()
+
         if block < nseq - 1:
             total = total + rbuf[block].astype(F32)
-    far_first(lambda step: back_copy(step).start())
     cbuf[me] = pbuf[me]
     hop(second[0], 3)
     hop(second[1], 1)

time: 72.3 us -> 71.8 us (level)
  no operation moved by 1% of the time
where the time goes in v5:
time: 71.8 us
  Pallas kernels  70.8 us (99%)
  local copies, waits for them, and re-layouts  0.97 us (1%)
    pallas_call x1, Pallas kernels, on_device(): pl.pallas_call(functools.partial(kernel, ny), out_shape=jax.ShapeDtypeStr...  70.8 us

profile of v5, /device:TPU:6, one launch (start us, length us, event | category | flops | bytes accessed | tf_op | source)
XLA Modules:
  0.0 71.8 jit_solution(776493462383689523)
XLA Ops:
  0.0 70.8 %layer.1 = bf16[256,2048]{1,0:T(8,128)(2,1)S(1)} custom-call(bf16[256,2048]{1,0:T(8,128)(2,1)} %tok_hbm.1, bf16[3,2048,512]{2,1,0:T(8,128)(2,1)} %bitcast.3, bf16[4,8,16,2048]{3,2,1,0:T(8,128)(2,1)} %bitcast.4, f32[32,16,128]{2,1,0:T(8,128)} %bitcast.5), custom_call_target="tpu_custom_call" | custom-call | tf_op jit(solution)/shard_map/layer/pallas_call | solution.py:546
  70.8 1.0 %copy.6 = bf16[256,2048]{1,0:T(8,128)(2,1)} copy(bf16[256,2048]{1,0:T(8,128)(2,1)S(1)} %layer.1) | data formatting | bytes 2097152
